TPU v7x, 32 devices: a whole 2x2x4 slice. The times are simulated.
32 devices in a mesh: section: 4 (over x, core), tp: 8 (over z, y).
Axes of the slice: x: 2, y: 2, z: 4, core: 2. Of those that a mesh axis runs over, the one named last changes fastest.
Arguments:
- patches: bfloat16 [2, 32, 4096], P(None, None, 'tp'), may hold values from -6 to 6
- table_ids: int32 [2, 32], replicated, may hold values from 0 to 32767
- lengths: int32 [2, 2], replicated, may hold values from 16 to 32
- embed_table: bfloat16 [32768, 4096], P('section', 'tp'), may hold values from -6 to 6
- norm_gain: bfloat16 [4, 4096], P('section'), may hold values from 0.099609375 to 1.8984375
- w_query: bfloat16 [4, 4096, 4096], P('section', None, 'tp'), may hold values from -0.09375 to 0.09375
- w_key: bfloat16 [4, 4096, 4096], P('section', None, 'tp'), may hold values from -0.09375 to 0.09375
- w_value: bfloat16 [4, 4096, 4096], P('section', None, 'tp'), may hold values from -0.09375 to 0.09375
- w_out: bfloat16 [4, 4096, 4096], P('section', None, 'tp'), may hold values from -0.09375 to 0.09375
Outputs:
- layer_rows: bfloat16 [4, 2, 32, 4096], P('section', None, None, 'tp')
Inputs may be any that keep to these rules, and one draw needn't show every extreme that they name: `lengths`: column 0 counts a micro-batch's valid patches, column 1 its valid table tokens.
All inputs are finite; a program needn't handle non-finite values.
Results may differ from a plain program's by a relative error of at most 0.01.
Values may be sent and summed in bfloat16 or wider, within the bound.
No kernel may reach another device: no remote copies, remote signals or barrier semaphores. Data moves between devices by JAX's collectives and lax.ppermute only.
A program may use at most 64 MiB of HBM per device.

v0:
```python
import math
import jax
import jax.numpy as jnp
from jax import lax
from jax.sharding import PartitionSpec as P

HEADS = 32
epsilon = 1e-06


def shifted(block, axis, distance):
    devices = range(lax.axis_size(axis))
    route = [(i - distance, i) for i in devices if i - distance in devices]
    return lax.ppermute(block, axis, route)


def local(patches, table_ids, lengths, embed_table, norm_gain, w_query, w_key, w_value, w_out):
    section_count = lax.axis_size("section")
    section_index = lax.axis_index("section")
    is_encoder = section_index < section_count // 2
    micro_count, row_count, width_local = patches.shape
    width_full = w_query.shape[1]
    head_dim = width_full // HEADS
    heads_local = width_local // head_dim
    score_scale = 1.0 / math.sqrt(head_dim)
    query_weight = w_query[0]
    key_weight = w_key[0]
    value_weight = w_value[0]
    out_weight = w_out[0]
    gain_row = norm_gain[0].astype(jnp.float32)
    vocab_local = embed_table.shape[0]
    local_ids = table_ids.reshape(-1) - section_index * vocab_local
    vocab_cols = lax.broadcasted_iota(jnp.int32, (local_ids.shape[0], vocab_local), 1)
    one_hot = (local_ids[:, None] == vocab_cols).astype(jnp.bfloat16)
    looked_up = jnp.dot(one_hot, embed_table, preferred_element_type=jnp.float32)
    embedded = lax.psum(looked_up.astype(jnp.bfloat16), "section")
    embedded = embedded.reshape(micro_count, row_count, width_local)
    first_inputs = jnp.concatenate([patches, embedded], axis=1)
    query_pos = lax.broadcasted_iota(jnp.int32, (row_count, 2 * row_count), 0)
    key_pos = lax.broadcasted_iota(jnp.int32, (row_count, 2 * row_count), 1)

    def head_outputs(full_rows, batch_index):
        values_f = full_rows.astype(jnp.float32)
        inverse = lax.rsqrt(jnp.mean(values_f * values_f, axis=-1, keepdims=True) + epsilon)
        normed = (values_f * inverse * gain_row).astype(jnp.bfloat16)
        own_rows = jnp.where(is_encoder, normed[:row_count], normed[row_count:])
        query = (
            jnp.dot(own_rows, query_weight, preferred_element_type=jnp.float32) * score_scale
        ).astype(jnp.bfloat16)
        key_rows = jnp.dot(normed, key_weight, preferred_element_type=jnp.float32).astype(
            jnp.bfloat16
        )
        value_rows = jnp.dot(normed, value_weight, preferred_element_type=jnp.float32).astype(
            jnp.bfloat16
        )
        query_heads = query.reshape(row_count, heads_local, head_dim)
        key_heads = key_rows.reshape(2 * row_count, heads_local, head_dim)
        value_heads = value_rows.reshape(2 * row_count, heads_local, head_dim)
        scores = jnp.einsum(
            "qhd,khd->hqk", query_heads, key_heads, preferred_element_type=jnp.float32
        )
        patch_count = lengths[batch_index, 0]
        table_count = lengths[batch_index, 1]
        patch_mask = (key_pos < row_count) & (key_pos < patch_count)
        table_mask = (
            (key_pos >= row_count)
            & (key_pos - row_count <= query_pos)
            & (key_pos - row_count < table_count)
        )
        key_mask = jnp.where(is_encoder, patch_mask, patch_mask | table_mask)
        exp_scores = jnp.where(key_mask[None], jnp.exp(scores), 0.0)
        weights = (exp_scores / jnp.sum(exp_scores, axis=-1, keepdims=True)).astype(jnp.bfloat16)
        head_mix = jnp.einsum(
            "hqk,khd->qhd", weights, value_heads, preferred_element_type=jnp.float32
        )
        return head_mix.astype(jnp.bfloat16).reshape(row_count, width_local)

    def add_block(piece):
        return jnp.dot(piece, out_weight, preferred_element_type=jnp.float32)

    def project_heads(head_mix):
        return add_block(lax.all_gather(head_mix, "tp", axis=1, tiled=True))

    def pass_on(stream):
        return shifted(stream, "section", 1)

    def place_rows(stream, updated):
        with_patches = jnp.concatenate([updated, stream[row_count:]], axis=0)
        with_table = jnp.concatenate([stream[:row_count], updated], axis=0)
        return jnp.where(is_encoder, with_patches, with_table)

    stash = jnp.zeros((micro_count, row_count, width_local), jnp.bfloat16)
    step_count = micro_count + section_count - 1

    def advance(step_index, carry):
        incoming, stash_rows = carry
        batch_index = step_index - section_index
        active = (batch_index >= 0) & (batch_index < micro_count)
        batch_index = jnp.clip(batch_index, 0, micro_count - 1)
        first_input = lax.dynamic_index_in_dim(first_inputs, batch_index, 0, keepdims=False)
        stream = jnp.where(section_index == 0, first_input, incoming)
        full_rows = lax.all_gather(stream, "tp", axis=1, tiled=True)
        change = project_heads(head_outputs(full_rows, batch_index))
        residual = jnp.where(is_encoder, stream[:row_count], stream[row_count:])
        updated = (residual.astype(jnp.float32) + change).astype(jnp.bfloat16)
        stored = lax.dynamic_update_index_in_dim(stash_rows, updated, batch_index, 0)
        stash_rows = jnp.where(active, stored, stash_rows)
        return (pass_on(place_rows(stream, updated)), stash_rows)

    start_stream = jnp.zeros((2 * row_count, width_local), jnp.bfloat16)
    final_carry = lax.fori_loop(0, step_count, advance, (start_stream, stash))
    return final_carry[1][None]


def solution(mesh):
    return jax.shard_map(
        local,
        mesh=mesh,
        in_specs=(
            P(None, None, "tp"),
            P(),
            P(),
            P("section", "tp"),
            P("section", None),
            P("section", None, "tp"),
            P("section", None, "tp"),
            P("section", None, "tp"),
            P("section", None, "tp"),
        ),
        out_specs=P("section", None, None, "tp"),
        check_vma=False,
    )
```

profile of v0, /device:TPU:1, one launch (start us, length us, event | category | flops | bytes accessed | tf_op | source)
XLA Modules:
  0.0 446.4 jit_solution(11587463912320818533)
XLA Ops:
  6.5 0.7 broadcast_subtract_fusion
  7.3 5.7 %fusion.32 = bf16[64,512]{1,0:T(8,128)(2,1)} fusion(bf16[8192,512]{1,0:T(8,128)(2,1)} %param.14, s32[64]{0:T(128)S(1)} %sub.33), kind=kOutput, calls=%fused_computation.52 | convolution fusion | flops 537427968 | bytes 8454400 | tf_op jit(solution)/shard_map/dot_general | solution.py:35
  13.0 32.2 %all-reduce.2.cloned.1.call-done = bf16[2,32,512]{2,1,0:T(8,128)(2,1)} async-done(((bf16[2,32,512]{2,1,0:T(8,128)(2,1)}), bf16[2,32,512]{2,1,0:T(8,128)(2,1)}) %all-reduce.2.cloned.1.call-update) | async-done | bytes 65552 | tf_op jit(solution)/shard_map/psum | solution.py:36
  45.3 0.8 pad_maximum_fusion
  46.2 392.8 %while.19 = (s32[]{:T(128)}, bf16[64,512]{1,0:T(8,128)(2,1)S(1)}, bf16[2,32,512]{2,1,0:T(8,128)(2,1)S(1)}, pred[]{:T(512)}, pred[]{:T(512)}, /*index=5*/s32[]{:T...) while((s32[]{:T(128)}, bf16[64,512]{1,0:T(8,128)(2,1)S(1)}, ...), condition=%wide.region_4.5_spmd.clone.clone, body=%wide.region_1.4_spmd.clone.clone.sunk | while | flops 812038400 | bytes 56055120 | solution.py:111
  46.2 25.8 %all_gather.26 = bf16[64,4096]{1,0:T(8,128)(2,1)S(1)} all-gather(bf16[64,512]{1,0:T(8,128)(2,1)S(1)} %bitcast_select_fusion.3), channel_id=1, replica_groups=mesh['section'=4,'tp'=8] {'tp'}, dimensions={1}, use_global_device_ids=true | all-gather | bytes 589824 | tf_op jit(solution)/shard_map/while/body/eval_jaxpr/all_gather | solution.py:102
  72.0 0.2 fusion.76
  72.2 0.6 constant_dynamic-slice_fusion.3
  73.0 3.2 fusion.79
  76.2 0.8 fusion.78
  77.1 0.8 fusion.80
  77.9 1.2 or_select_fusion.2
  79.3 0.2 fusion.82
  79.5 24.6 %all_gather.27 = bf16[32,4096]{1,0:T(8,128)(2,1)S(1)} all-gather(bf16[32,512]{1,0:T(8,128)(2,1)S(1)} %bitcast.89), channel_id=1, replica_groups=mesh['section'=4,'tp'=8] {'tp'}, dimensions={1}, use_global_device_ids=true | all-gather | bytes 294912 | tf_op jit(solution)/shard_map/while/body/eval_jaxpr/all_gather | solution.py:82
  104.1 3.0 fusion.83
  107.2 15.9 %collective-permute-start = (bf16[64,512]{1,0:T(8,128)(2,1)S(1)}, bf16[64,512]{1,0:T(8,128)(2,1)S(1)}, u32[]{:S(2)}, u32[]{:S(2)}) collective-permute-start(bf16[64,512]{1,0:T(8,128)(2,1)S(1)} %maximum_select_fusion.2), channel_id=1, source_target_pairs={{0,8},{8,16},{16,24},{1,9},{9,17},{17,25},{2,10},{10,18},{18,26},{... | collective-permute-start | bytes 196616 | tf_op jit(solution)/shard_map/while/body/eval_jaxpr/ppermute | solution.py:14
  123.1 1.3 collective-permute-done
  124.4 25.8 %all_gather.26 = bf16[64,4096]{1,0:T(8,128)(2,1)S(1)} all-gather(bf16[64,512]{1,0:T(8,128)(2,1)S(1)} %bitcast_select_fusion.3), channel_id=1, replica_groups=mesh['section'=4,'tp'=8] {'tp'}, dimensions={1}, use_global_device_ids=true | all-gather | bytes 589824 | tf_op jit(solution)/shard_map/while/body/eval_jaxpr/all_gather | solution.py:102
  150.2 0.2 fusion.76
  150.4 0.6 constant_dynamic-slice_fusion.3
  151.2 3.2 fusion.79
  154.4 0.8 fusion.78
  155.2 0.8 fusion.80
  156.0 1.2 or_select_fusion.2
  157.4 0.2 fusion.82
  157.7 24.6 %all_gather.27 = bf16[32,4096]{1,0:T(8,128)(2,1)S(1)} all-gather(bf16[32,512]{1,0:T(8,128)(2,1)S(1)} %bitcast.89), channel_id=1, replica_groups=mesh['section'=4,'tp'=8] {'tp'}, dimensions={1}, use_global_device_ids=true | all-gather | bytes 294912 | tf_op jit(solution)/shard_map/while/body/eval_jaxpr/all_gather | solution.py:82
  182.3 3.0 fusion.83
  185.3 16.4 %collective-permute-start = (bf16[64,512]{1,0:T(8,128)(2,1)S(1)}, bf16[64,512]{1,0:T(8,128)(2,1)S(1)}, u32[]{:S(2)}, u32[]{:S(2)}) collective-permute-start(bf16[64,512]{1,0:T(8,128)(2,1)S(1)} %maximum_select_fusion.2), channel_id=1, source_target_pairs={{0,8},{8,16},{16,24},{1,9},{9,17},{17,25},{2,10},{10,18},{18,26},{... | collective-permute-start | bytes 196616 | tf_op jit(solution)/shard_map/while/body/eval_jaxpr/ppermute | solution.py:14
  201.7 1.3 collective-permute-done
  203.1 25.5 %all_gather.26 = bf16[64,4096]{1,0:T(8,128)(2,1)S(1)} all-gather(bf16[64,512]{1,0:T(8,128)(2,1)S(1)} %bitcast_select_fusion.3), channel_id=1, replica_groups=mesh['section'=4,'tp'=8] {'tp'}, dimensions={1}, use_global_device_ids=true | all-gather | bytes 589824 | tf_op jit(solution)/shard_map/while/body/eval_jaxpr/all_gather | solution.py:102
  228.6 0.2 fusion.76
  228.8 0.6 constant_dynamic-slice_fusion.3
  229.6 3.2 fusion.79
  232.8 0.8 fusion.78
  233.6 0.8 fusion.80
  234.4 1.2 or_select_fusion.2
  235.8 0.2 fusion.82
  236.1 24.5 %all_gather.27 = bf16[32,4096]{1,0:T(8,128)(2,1)S(1)} all-gather(bf16[32,512]{1,0:T(8,128)(2,1)S(1)} %bitcast.89), channel_id=1, replica_groups=mesh['section'=4,'tp'=8] {'tp'}, dimensions={1}, use_global_device_ids=true | all-gather | bytes 294912 | tf_op jit(solution)/shard_map/while/body/eval_jaxpr/all_gather | solution.py:82
  260.6 3.0 fusion.83
  263.7 16.6 %collective-permute-start = (bf16[64,512]{1,0:T(8,128)(2,1)S(1)}, bf16[64,512]{1,0:T(8,128)(2,1)S(1)}, u32[]{:S(2)}, u32[]{:S(2)}) collective-permute-start(bf16[64,512]{1,0:T(8,128)(2,1)S(1)} %maximum_select_fusion.2), channel_id=1, source_target_pairs={{0,8},{8,16},{16,24},{1,9},{9,17},{17,25},{2,10},{10,18},{18,26},{... | collective-permute-start | bytes 196616 | tf_op jit(solution)/shard_map/while/body/eval_jaxpr/ppermute | solution.py:14
  280.3 1.3 collective-permute-done
  281.6 25.5 %all_gather.26 = bf16[64,4096]{1,0:T(8,128)(2,1)S(1)} all-gather(bf16[64,512]{1,0:T(8,128)(2,1)S(1)} %bitcast_select_fusion.3), channel_id=1, replica_groups=mesh['section'=4,'tp'=8] {'tp'}, dimensions={1}, use_global_device_ids=true | all-gather | bytes 589824 | tf_op jit(solution)/shard_map/while/body/eval_jaxpr/all_gather | solution.py:102
  307.4 0.6 constant_dynamic-slice_fusion.3
  308.2 3.2 fusion.79
  311.4 0.8 fusion.78
  312.2 0.8 fusion.80
  313.0 1.2 or_select_fusion.2
  314.4 0.2 fusion.82
  314.7 24.7 %all_gather.27 = bf16[32,4096]{1,0:T(8,128)(2,1)S(1)} all-gather(bf16[32,512]{1,0:T(8,128)(2,1)S(1)} %bitcast.89), channel_id=1, replica_groups=mesh['section'=4,'tp'=8] {'tp'}, dimensions={1}, use_global_device_ids=true | all-gather | bytes 294912 | tf_op jit(solution)/shard_map/while/body/eval_jaxpr/all_gather | solution.py:82
  339.4 3.0 fusion.83
  342.4 16.5 %collective-permute-start = (bf16[64,512]{1,0:T(8,128)(2,1)S(1)}, bf16[64,512]{1,0:T(8,128)(2,1)S(1)}, u32[]{:S(2)}, u32[]{:S(2)}) collective-permute-start(bf16[64,512]{1,0:T(8,128)(2,1)S(1)} %maximum_select_fusion.2), channel_id=1, source_target_pairs={{0,8},{8,16},{16,24},{1,9},{9,17},{17,25},{2,10},{10,18},{18,26},{... | collective-permute-start | bytes 196616 | tf_op jit(solution)/shard_map/while/body/eval_jaxpr/ppermute | solution.py:14
  358.9 1.3 collective-permute-done
  360.2 25.4 %all_gather.26 = bf16[64,4096]{1,0:T(8,128)(2,1)S(1)} all-gather(bf16[64,512]{1,0:T(8,128)(2,1)S(1)} %bitcast_select_fusion.3), channel_id=1, replica_groups=mesh['section'=4,'tp'=8] {'tp'}, dimensions={1}, use_global_device_ids=true | all-gather | bytes 589824 | tf_op jit(solution)/shard_map/while/body/eval_jaxpr/all_gather | solution.py:102
  385.8 0.6 constant_dynamic-slice_fusion.3
  386.6 3.2 fusion.79
  389.8 0.8 fusion.78
  390.7 0.8 fusion.80
  391.5 1.2 or_select_fusion.2
  392.9 0.2 fusion.82
  393.1 25.0 %all_gather.27 = bf16[32,4096]{1,0:T(8,128)(2,1)S(1)} all-gather(bf16[32,512]{1,0:T(8,128)(2,1)S(1)} %bitcast.89), channel_id=1, replica_groups=mesh['section'=4,'tp'=8] {'tp'}, dimensions={1}, use_global_device_ids=true | all-gather | bytes 294912 | tf_op jit(solution)/shard_map/while/body/eval_jaxpr/all_gather | solution.py:82
  418.1 3.0 fusion.83
  421.2 16.4 %collective-permute-start = (bf16[64,512]{1,0:T(8,128)(2,1)S(1)}, bf16[64,512]{1,0:T(8,128)(2,1)S(1)}, u32[]{:S(2)}, u32[]{:S(2)}) collective-permute-start(bf16[64,512]{1,0:T(8,128)(2,1)S(1)} %maximum_select_fusion.2), channel_id=1, source_target_pairs={{0,8},{8,16},{16,24},{1,9},{9,17},{17,25},{2,10},{10,18},{18,26},{... | collective-permute-start | bytes 196616 | tf_op jit(solution)/shard_map/while/body/eval_jaxpr/ppermute | solution.py:14
  437.6 1.3 collective-permute-done
  438.9 0.6 copy-done.2
  (70 shorter events, 2.6 us)
Async XLA Ops:
  6.5 38.7 %all-reduce.2.cloned.1.call-start = ((), (), s32[]{:S(2)}) async-start(), calls=%async_computation | async-start | bytes 131072 | tf_op jit(solution)/shard_map/psum | solution.py:36
  7.3 5.7 %copy-start.5 = (bf16[1,4096]{1,0:T(2,128)(2,1)S(1)}, bf16[1,4096]{1,0:T(2,128)(2,1)}, u32[]{:S(2)}) copy-start(bf16[1,4096]{1,0:T(2,128)(2,1)} %param.15) | copy-start | bytes 24580
  7.3 38.0 %copy-start.3 = (bf16[2,32,512]{2,1,0:T(8,128)(2,1)S(1)}, bf16[2,32,512]{2,1,0:T(8,128)(2,1)}, u32[]{:S(2)}) copy-start(bf16[2,32,512]{2,1,0:T(8,128)(2,1)} %param.11) | copy-start | bytes 196612
  7.3 38.8 %copy-start.4 = (s32[2,2]{1,0:T(2,128)S(1)}, s32[2,2]{1,0:T(2,128)}, u32[]{:S(2)}) copy-start(s32[2,2]{1,0:T(2,128)} %param.13) | copy-start | bytes 52
  46.2 30.0 %copy-start = (bf16[4096,512]{1,0:T(8,128)(2,1)S(1)}, bf16[4096,512]{1,0:T(8,128)(2,1)}, u32[]{:S(2)}) copy-start(bf16[4096,512]{1,0:T(8,128)(2,1)} %get-tuple-element.579) | copy-start | bytes 12582916 | tf_op jit(solution)/shard_map/while
  73.0 4.0 copy-start.1
  107.2 17.2 %collective-permute-start = (bf16[64,512]{1,0:T(8,128)(2,1)S(1)}, bf16[64,512]{1,0:T(8,128)(2,1)S(1)}, u32[]{:S(2)}, u32[]{:S(2)}) collective-permute-start(bf16[64,512]{1,0:T(8,128)(2,1)S(1)} %maximum_select_fusion.2), channel_id=1, source_target_pairs={{0,8},{8,16},{16,24},{1,9},{9,17},{17,25},{2,10},{10,18},{18,26},{... | collective-permute-start | bytes 196616 | tf_op jit(solution)/shard_map/while/body/eval_jaxpr/ppermute | solution.py:14
  124.4 30.0 %copy-start = (bf16[4096,512]{1,0:T(8,128)(2,1)S(1)}, bf16[4096,512]{1,0:T(8,128)(2,1)}, u32[]{:S(2)}) copy-start(bf16[4096,512]{1,0:T(8,128)(2,1)} %get-tuple-element.579) | copy-start | bytes 12582916 | tf_op jit(solution)/shard_map/while
  151.2 4.0 copy-start.1
  185.3 17.7 %collective-permute-start = (bf16[64,512]{1,0:T(8,128)(2,1)S(1)}, bf16[64,512]{1,0:T(8,128)(2,1)S(1)}, u32[]{:S(2)}, u32[]{:S(2)}) collective-permute-start(bf16[64,512]{1,0:T(8,128)(2,1)S(1)} %maximum_select_fusion.2), channel_id=1, source_target_pairs={{0,8},{8,16},{16,24},{1,9},{9,17},{17,25},{2,10},{10,18},{18,26},{... | collective-permute-start | bytes 196616 | tf_op jit(solution)/shard_map/while/body/eval_jaxpr/ppermute | solution.py:14
  203.0 29.7 %copy-start = (bf16[4096,512]{1,0:T(8,128)(2,1)S(1)}, bf16[4096,512]{1,0:T(8,128)(2,1)}, u32[]{:S(2)}) copy-start(bf16[4096,512]{1,0:T(8,128)(2,1)} %get-tuple-element.579) | copy-start | bytes 12582916 | tf_op jit(solution)/shard_map/while
  229.6 4.0 copy-start.1
  263.7 17.9 %collective-permute-start = (bf16[64,512]{1,0:T(8,128)(2,1)S(1)}, bf16[64,512]{1,0:T(8,128)(2,1)S(1)}, u32[]{:S(2)}, u32[]{:S(2)}) collective-permute-start(bf16[64,512]{1,0:T(8,128)(2,1)S(1)} %maximum_select_fusion.2), channel_id=1, source_target_pairs={{0,8},{8,16},{16,24},{1,9},{9,17},{17,25},{2,10},{10,18},{18,26},{... | collective-permute-start | bytes 196616 | tf_op jit(solution)/shard_map/while/body/eval_jaxpr/ppermute | solution.py:14
  281.6 29.8 %copy-start = (bf16[4096,512]{1,0:T(8,128)(2,1)S(1)}, bf16[4096,512]{1,0:T(8,128)(2,1)}, u32[]{:S(2)}) copy-start(bf16[4096,512]{1,0:T(8,128)(2,1)} %get-tuple-element.579) | copy-start | bytes 12582916 | tf_op jit(solution)/shard_map/while
  308.2 4.0 copy-start.1
  342.4 17.8 %collective-permute-start = (bf16[64,512]{1,0:T(8,128)(2,1)S(1)}, bf16[64,512]{1,0:T(8,128)(2,1)S(1)}, u32[]{:S(2)}, u32[]{:S(2)}) collective-permute-start(bf16[64,512]{1,0:T(8,128)(2,1)S(1)} %maximum_select_fusion.2), channel_id=1, source_target_pairs={{0,8},{8,16},{16,24},{1,9},{9,17},{17,25},{2,10},{10,18},{18,26},{... | collective-permute-start | bytes 196616 | tf_op jit(solution)/shard_map/while/body/eval_jaxpr/ppermute | solution.py:14
  360.2 29.6 %copy-start = (bf16[4096,512]{1,0:T(8,128)(2,1)S(1)}, bf16[4096,512]{1,0:T(8,128)(2,1)}, u32[]{:S(2)}) copy-start(bf16[4096,512]{1,0:T(8,128)(2,1)} %get-tuple-element.579) | copy-start | bytes 12582916 | tf_op jit(solution)/shard_map/while
  386.6 4.0 copy-start.1
  421.2 17.7 %collective-permute-start = (bf16[64,512]{1,0:T(8,128)(2,1)S(1)}, bf16[64,512]{1,0:T(8,128)(2,1)S(1)}, u32[]{:S(2)}, u32[]{:S(2)}) collective-permute-start(bf16[64,512]{1,0:T(8,128)(2,1)S(1)} %maximum_select_fusion.2), channel_id=1, source_target_pairs={{0,8},{8,16},{16,24},{1,9},{9,17},{17,25},{2,10},{10,18},{18,26},{... | collective-permute-start | bytes 196616 | tf_op jit(solution)/shard_map/while/body/eval_jaxpr/ppermute | solution.py:14
  438.9 0.6 copy-start.2
Sparse Core Ops, SparseCore 0:
  13.1 32.1 all-reduce.1
where the time goes:
time: 447 us; the launch traced here: 446 us
  blocking collectives  252 us (56%)
  starting transfers between devices  81.8 us (18%)
  matrix products  46.6 us (10%)
  waiting for transfers between devices  38.8 us (9%)
  between operations  13.4 us (3%)
  other arithmetic  9.88 us (2%)
    all_gather x5, blocking collectives, advance(): full_rows = lax.all_gather(stream, 'tp', axis=1, tiled=True)  128 us
    all_gather x5, blocking collectives, project_heads(): return add_block(lax.all_gather(head_mix, 'tp', axis=1, tiled=True))  124 us
    ppermute x5, starting transfers between devices, shifted(): return lax.ppermute(block, axis, route)  81.8 us
    psum x1, waiting for transfers between devices, local(): embedded = lax.psum(looked_up.astype(jnp.bfloat16), 'section')  32.2 us
    dot_general x5, matrix products, head_outputs(): jnp.dot(normed, key_weight, preferred_element_type=jnp.float32)  15.9 us
    dot_general x5, matrix products, add_block(): return jnp.dot(piece, out_weight, preferred_element_type=jnp.float32)  15 us
  transfers between devices with their start and end apart: 6, of which 6 were waited for; matrix products, arithmetic and copies ran while one was open for 0% of the time, Pallas kernels for 0%

commit v1 on v0

--- a/solution.py
+++ b/solution.py
@@ -33,7 +33,7 @@
     vocab_cols = lax.broadcasted_iota(jnp.int32, (local_ids.shape[0], vocab_local), 1)
     one_hot = (local_ids[:, None] == vocab_cols).astype(jnp.bfloat16)
     looked_up = jnp.dot(one_hot, embed_table, preferred_element_type=jnp.float32)
-    embedded = lax.psum(looked_up.astype(jnp.bfloat16), "section")
+    embedded = jnp.sum(lax.all_gather(looked_up.astype(jnp.bfloat16), "section"), axis=0)
     embedded = embedded.reshape(micro_count, row_count, width_local)
     first_inputs = jnp.concatenate([patches, embedded], axis=1)
     query_pos = lax.broadcasted_iota(jnp.int32, (row_count, 2 * row_count), 0)

time: 447 us -> 407 us (0.911)
  waiting for transfers between devices: 38.8 us -> 6.53 us
  between operations: 13.4 us -> 0.08 us
  blocking collectives: 252 us -> 259 us
    psum x1 -> x0, waiting for transfers between devices: 32.2 us -> none  [local(): embedded = lax.psum(looked_up.astype(jnp.bfloat16), 'section')]
    all_gather x0 -> x1, blocking collectives: none -> 7.07 us  [local(): lax.all_gather(looked_up.astype(jnp.bfloat16), 'section')]
  transfers between devices with their start and end apart: 6 -> 5, of which waited for: 6 -> 5; matrix products, arithmetic and copies ran while one was open for 0% -> 0% of each run, Pallas kernels for 0% -> 0%
where the time goes in v1:
time: 407 us; the launch traced here: 406 us
  blocking collectives  259 us (64%)
  starting transfers between devices  81.2 us (20%)
  matrix products  46 us (11%)
  other arithmetic  9.29 us (2%)
  waiting for transfers between devices  6.53 us (2%)
  local copies, waits for them, and re-layouts  4.21 us (1%)
    all_gather x5, blocking collectives, advance(): full_rows = lax.all_gather(stream, 'tp', axis=1, tiled=True)  128 us
    all_gather x5, blocking collectives, project_heads(): return add_block(lax.all_gather(head_mix, 'tp', axis=1, tiled=True))  124 us
    ppermute x5, starting transfers between devices, shifted(): return lax.ppermute(block, axis, route)  81.2 us
    dot_general x5, matrix products, head_outputs(): jnp.dot(normed, key_weight, preferred_element_type=jnp.float32)  15.9 us
    dot_general x5, matrix products, add_block(): return jnp.dot(piece, out_weight, preferred_element_type=jnp.float32)  15 us
  transfers between devices with their start and end apart: 5, of which 5 were waited for; matrix products, arithmetic and copies ran while one was open for 0% of the time, Pallas kernels for 0%

profile of v1, /device:TPU:1, one launch (start us, length us, event | category | flops | bytes accessed | tf_op | source)
XLA Modules:
  0.0 406.5 jit_solution(18373605136341013338)
XLA Ops:
  0.0 0.7 broadcast_subtract_fusion
  0.8 5.0 %fusion.32 = bf16[64,512]{1,0:T(8,128)(2,1)S(1)} fusion(bf16[8192,512]{1,0:T(8,128)(2,1)} %param.14, s32[64]{0:T(128)S(1)} %sub.33), kind=kOutput, calls=%fused_computation.52 | convolution fusion | flops 537427968 | bytes 8454400 | tf_op jit(solution)/shard_map/dot_general | solution.py:35
  5.8 7.1 %all-gather = bf16[256,512]{1,0:T(8,128)(2,1)S(1)} all-gather(bf16[64,512]{1,0:T(8,128)(2,1)S(1)} %fusion.32), channel_id=2, replica_groups=mesh['section'=4,'tp'=8] {'section'}, dimensions={0}, use_global_device_ids=true | all-gather | bytes 327680 | tf_op jit(solution)/shard_map/all_gather | solution.py:36
  13.0 392.8 %while.19 = (s32[]{:T(128)}, bf16[64,512]{1,0:T(8,128)(2,1)S(1)}, bf16[2,32,512]{2,1,0:T(8,128)(2,1)S(1)}, pred[]{:T(512)}, pred[]{:T(512)}, /*index=5*/s32[]{:T...) while((s32[]{:T(128)}, bf16[64,512]{1,0:T(8,128)(2,1)S(1)}, ...), condition=%wide.region_4.5_spmd.clone.clone, body=%wide.region_1.4_spmd.clone.clone.sunk | while | flops 812038400 | bytes 56055120 | solution.py:111
  13.1 25.7 %all_gather.34 = bf16[64,4096]{1,0:T(8,128)(2,1)S(1)} all-gather(bf16[64,512]{1,0:T(8,128)(2,1)S(1)} %bitcast_select_fusion.3), channel_id=1, replica_groups=mesh['section'=4,'tp'=8] {'tp'}, dimensions={1}, use_global_device_ids=true | all-gather | bytes 589824 | tf_op jit(solution)/shard_map/while/body/eval_jaxpr/all_gather | solution.py:102
  38.8 0.2 fusion.76
  39.1 0.7 constant_dynamic-slice_fusion.3
  39.9 3.2 fusion.79
  43.1 0.8 fusion.78
  44.0 0.8 fusion.80
  44.8 1.3 or_select_fusion.2
  46.2 0.2 fusion.82
  46.5 24.4 %all_gather.35 = bf16[32,4096]{1,0:T(8,128)(2,1)S(1)} all-gather(bf16[32,512]{1,0:T(8,128)(2,1)S(1)} %bitcast.90), channel_id=1, replica_groups=mesh['section'=4,'tp'=8] {'tp'}, dimensions={1}, use_global_device_ids=true | all-gather | bytes 294912 | tf_op jit(solution)/shard_map/while/body/eval_jaxpr/all_gather | solution.py:82
  70.9 3.0 fusion.83
  73.9 15.8 %collective-permute-start = (bf16[64,512]{1,0:T(8,128)(2,1)S(1)}, bf16[64,512]{1,0:T(8,128)(2,1)S(1)}, u32[]{:S(2)}, u32[]{:S(2)}) collective-permute-start(bf16[64,512]{1,0:T(8,128)(2,1)S(1)} %maximum_select_fusion.2), channel_id=1, source_target_pairs={{0,8},{8,16},{16,24},{1,9},{9,17},{17,25},{2,10},{10,18},{18,26},{... | collective-permute-start | bytes 196616 | tf_op jit(solution)/shard_map/while/body/eval_jaxpr/ppermute | solution.py:14
  89.8 1.3 collective-permute-done
  91.1 25.9 %all_gather.34 = bf16[64,4096]{1,0:T(8,128)(2,1)S(1)} all-gather(bf16[64,512]{1,0:T(8,128)(2,1)S(1)} %bitcast_select_fusion.3), channel_id=1, replica_groups=mesh['section'=4,'tp'=8] {'tp'}, dimensions={1}, use_global_device_ids=true | all-gather | bytes 589824 | tf_op jit(solution)/shard_map/while/body/eval_jaxpr/all_gather | solution.py:102
  117.0 0.2 fusion.76
  117.2 0.7 constant_dynamic-slice_fusion.3
  118.1 3.2 fusion.79
  121.3 0.8 fusion.78
  122.1 0.8 fusion.80
  122.9 1.3 or_select_fusion.2
  124.4 0.2 fusion.82
  124.6 24.4 %all_gather.35 = bf16[32,4096]{1,0:T(8,128)(2,1)S(1)} all-gather(bf16[32,512]{1,0:T(8,128)(2,1)S(1)} %bitcast.90), channel_id=1, replica_groups=mesh['section'=4,'tp'=8] {'tp'}, dimensions={1}, use_global_device_ids=true | all-gather | bytes 294912 | tf_op jit(solution)/shard_map/while/body/eval_jaxpr/all_gather | solution.py:82
  149.1 3.0 fusion.83
  152.1 16.2 %collective-permute-start = (bf16[64,512]{1,0:T(8,128)(2,1)S(1)}, bf16[64,512]{1,0:T(8,128)(2,1)S(1)}, u32[]{:S(2)}, u32[]{:S(2)}) collective-permute-start(bf16[64,512]{1,0:T(8,128)(2,1)S(1)} %maximum_select_fusion.2), channel_id=1, source_target_pairs={{0,8},{8,16},{16,24},{1,9},{9,17},{17,25},{2,10},{10,18},{18,26},{... | collective-permute-start | bytes 196616 | tf_op jit(solution)/shard_map/while/body/eval_jaxpr/ppermute | solution.py:14
  168.3 1.3 collective-permute-done
  169.6 25.4 %all_gather.34 = bf16[64,4096]{1,0:T(8,128)(2,1)S(1)} all-gather(bf16[64,512]{1,0:T(8,128)(2,1)S(1)} %bitcast_select_fusion.3), channel_id=1, replica_groups=mesh['section'=4,'tp'=8] {'tp'}, dimensions={1}, use_global_device_ids=true | all-gather | bytes 589824 | tf_op jit(solution)/shard_map/while/body/eval_jaxpr/all_gather | solution.py:102
  195.1 0.2 fusion.76
  195.3 0.7 constant_dynamic-slice_fusion.3
  196.2 3.2 fusion.79
  199.4 0.8 fusion.78
  200.2 0.8 fusion.80
  201.0 1.3 or_select_fusion.2
  202.5 0.2 fusion.82
  202.7 24.9 %all_gather.35 = bf16[32,4096]{1,0:T(8,128)(2,1)S(1)} all-gather(bf16[32,512]{1,0:T(8,128)(2,1)S(1)} %bitcast.90), channel_id=1, replica_groups=mesh['section'=4,'tp'=8] {'tp'}, dimensions={1}, use_global_device_ids=true | all-gather | bytes 294912 | tf_op jit(solution)/shard_map/while/body/eval_jaxpr/all_gather | solution.py:82
  227.6 3.0 fusion.83
  230.6 16.5 %collective-permute-start = (bf16[64,512]{1,0:T(8,128)(2,1)S(1)}, bf16[64,512]{1,0:T(8,128)(2,1)S(1)}, u32[]{:S(2)}, u32[]{:S(2)}) collective-permute-start(bf16[64,512]{1,0:T(8,128)(2,1)S(1)} %maximum_select_fusion.2), channel_id=1, source_target_pairs={{0,8},{8,16},{16,24},{1,9},{9,17},{17,25},{2,10},{10,18},{18,26},{... | collective-permute-start | bytes 196616 | tf_op jit(solution)/shard_map/while/body/eval_jaxpr/ppermute | solution.py:14
  247.2 1.3 collective-permute-done
  248.5 25.5 %all_gather.34 = bf16[64,4096]{1,0:T(8,128)(2,1)S(1)} all-gather(bf16[64,512]{1,0:T(8,128)(2,1)S(1)} %bitcast_select_fusion.3), channel_id=1, replica_groups=mesh['section'=4,'tp'=8] {'tp'}, dimensions={1}, use_global_device_ids=true | all-gather | bytes 589824 | tf_op jit(solution)/shard_map/while/body/eval_jaxpr/all_gather | solution.py:102
  274.0 0.2 fusion.76
  274.2 0.7 constant_dynamic-slice_fusion.3
  275.1 3.2 fusion.79
  278.3 0.8 fusion.78
  279.1 0.8 fusion.80
  279.9 1.3 or_select_fusion.2
  281.4 0.2 fusion.82
  281.6 24.8 %all_gather.35 = bf16[32,4096]{1,0:T(8,128)(2,1)S(1)} all-gather(bf16[32,512]{1,0:T(8,128)(2,1)S(1)} %bitcast.90), channel_id=1, replica_groups=mesh['section'=4,'tp'=8] {'tp'}, dimensions={1}, use_global_device_ids=true | all-gather | bytes 294912 | tf_op jit(solution)/shard_map/while/body/eval_jaxpr/all_gather | solution.py:82
  306.4 3.0 fusion.83
  309.5 16.2 %collective-permute-start = (bf16[64,512]{1,0:T(8,128)(2,1)S(1)}, bf16[64,512]{1,0:T(8,128)(2,1)S(1)}, u32[]{:S(2)}, u32[]{:S(2)}) collective-permute-start(bf16[64,512]{1,0:T(8,128)(2,1)S(1)} %maximum_select_fusion.2), channel_id=1, source_target_pairs={{0,8},{8,16},{16,24},{1,9},{9,17},{17,25},{2,10},{10,18},{18,26},{... | collective-permute-start | bytes 196616 | tf_op jit(solution)/shard_map/while/body/eval_jaxpr/ppermute | solution.py:14
  325.7 1.3 collective-permute-done
  327.0 25.4 %all_gather.34 = bf16[64,4096]{1,0:T(8,128)(2,1)S(1)} all-gather(bf16[64,512]{1,0:T(8,128)(2,1)S(1)} %bitcast_select_fusion.3), channel_id=1, replica_groups=mesh['section'=4,'tp'=8] {'tp'}, dimensions={1}, use_global_device_ids=true | all-gather | bytes 589824 | tf_op jit(solution)/shard_map/while/body/eval_jaxpr/all_gather | solution.py:102
  352.6 0.7 constant_dynamic-slice_fusion.3
  353.5 3.2 fusion.79
  356.7 0.8 fusion.78
  357.6 0.8 fusion.80
  358.4 1.3 or_select_fusion.2
  359.8 0.2 fusion.82
  360.0 25.0 %all_gather.35 = bf16[32,4096]{1,0:T(8,128)(2,1)S(1)} all-gather(bf16[32,512]{1,0:T(8,128)(2,1)S(1)} %bitcast.90), channel_id=1, replica_groups=mesh['section'=4,'tp'=8] {'tp'}, dimensions={1}, use_global_device_ids=true | all-gather | bytes 294912 | tf_op jit(solution)/shard_map/while/body/eval_jaxpr/all_gather | solution.py:82
  385.0 3.0 fusion.83
  388.1 16.5 %collective-permute-start = (bf16[64,512]{1,0:T(8,128)(2,1)S(1)}, bf16[64,512]{1,0:T(8,128)(2,1)S(1)}, u32[]{:S(2)}, u32[]{:S(2)}) collective-permute-start(bf16[64,512]{1,0:T(8,128)(2,1)S(1)} %maximum_select_fusion.2), channel_id=1, source_target_pairs={{0,8},{8,16},{16,24},{1,9},{9,17},{17,25},{2,10},{10,18},{18,26},{... | collective-permute-start | bytes 196616 | tf_op jit(solution)/shard_map/while/body/eval_jaxpr/ppermute | solution.py:14
  404.6 1.3 collective-permute-done
  405.9 0.6 copy-done.2
  (69 shorter events, 2.4 us)
Async XLA Ops:
  0.8 12.2 %copy-start.3 = (bf16[2,32,512]{2,1,0:T(8,128)(2,1)S(1)}, bf16[2,32,512]{2,1,0:T(8,128)(2,1)}, u32[]{:S(2)}) copy-start(bf16[2,32,512]{2,1,0:T(8,128)(2,1)} %param.11) | copy-start | bytes 196612
  0.8 12.2 %copy-start.5 = (bf16[1,4096]{1,0:T(2,128)(2,1)S(1)}, bf16[1,4096]{1,0:T(2,128)(2,1)}, u32[]{:S(2)}) copy-start(bf16[1,4096]{1,0:T(2,128)(2,1)} %param.15) | copy-start | bytes 24580
  0.8 12.3 %copy-start.4 = (s32[2,2]{1,0:T(2,128)S(1)}, s32[2,2]{1,0:T(2,128)}, u32[]{:S(2)}) copy-start(s32[2,2]{1,0:T(2,128)} %param.13) | copy-start | bytes 52
  13.1 30.1 %copy-start = (bf16[4096,512]{1,0:T(8,128)(2,1)S(1)}, bf16[4096,512]{1,0:T(8,128)(2,1)}, u32[]{:S(2)}) copy-start(bf16[4096,512]{1,0:T(8,128)(2,1)} %get-tuple-element.579) | copy-start | bytes 12582916 | tf_op jit(solution)/shard_map/while
  39.9 4.0 copy-start.1
  73.9 17.1 %collective-permute-start = (bf16[64,512]{1,0:T(8,128)(2,1)S(1)}, bf16[64,512]{1,0:T(8,128)(2,1)S(1)}, u32[]{:S(2)}, u32[]{:S(2)}) collective-permute-start(bf16[64,512]{1,0:T(8,128)(2,1)S(1)} %maximum_select_fusion.2), channel_id=1, source_target_pairs={{0,8},{8,16},{16,24},{1,9},{9,17},{17,25},{2,10},{10,18},{18,26},{... | collective-permute-start | bytes 196616 | tf_op jit(solution)/shard_map/while/body/eval_jaxpr/ppermute | solution.py:14
  91.1 30.2 %copy-start = (bf16[4096,512]{1,0:T(8,128)(2,1)S(1)}, bf16[4096,512]{1,0:T(8,128)(2,1)}, u32[]{:S(2)}) copy-start(bf16[4096,512]{1,0:T(8,128)(2,1)} %get-tuple-element.579) | copy-start | bytes 12582916 | tf_op jit(solution)/shard_map/while
  118.1 4.0 copy-start.1
  152.1 17.5 %collective-permute-start = (bf16[64,512]{1,0:T(8,128)(2,1)S(1)}, bf16[64,512]{1,0:T(8,128)(2,1)S(1)}, u32[]{:S(2)}, u32[]{:S(2)}) collective-permute-start(bf16[64,512]{1,0:T(8,128)(2,1)S(1)} %maximum_select_fusion.2), channel_id=1, source_target_pairs={{0,8},{8,16},{16,24},{1,9},{9,17},{17,25},{2,10},{10,18},{18,26},{... | collective-permute-start | bytes 196616 | tf_op jit(solution)/shard_map/while/body/eval_jaxpr/ppermute | solution.py:14
  169.6 29.7 %copy-start = (bf16[4096,512]{1,0:T(8,128)(2,1)S(1)}, bf16[4096,512]{1,0:T(8,128)(2,1)}, u32[]{:S(2)}) copy-start(bf16[4096,512]{1,0:T(8,128)(2,1)} %get-tuple-element.579) | copy-start | bytes 12582916 | tf_op jit(solution)/shard_map/while
  196.2 4.0 copy-start.1
  230.6 17.8 %collective-permute-start = (bf16[64,512]{1,0:T(8,128)(2,1)S(1)}, bf16[64,512]{1,0:T(8,128)(2,1)S(1)}, u32[]{:S(2)}, u32[]{:S(2)}) collective-permute-start(bf16[64,512]{1,0:T(8,128)(2,1)S(1)} %maximum_select_fusion.2), channel_id=1, source_target_pairs={{0,8},{8,16},{16,24},{1,9},{9,17},{17,25},{2,10},{10,18},{18,26},{... | collective-permute-start | bytes 196616 | tf_op jit(solution)/shard_map/while/body/eval_jaxpr/ppermute | solution.py:14
  248.5 29.8 %copy-start = (bf16[4096,512]{1,0:T(8,128)(2,1)S(1)}, bf16[4096,512]{1,0:T(8,128)(2,1)}, u32[]{:S(2)}) copy-start(bf16[4096,512]{1,0:T(8,128)(2,1)} %get-tuple-element.579) | copy-start | bytes 12582916 | tf_op jit(solution)/shard_map/while
  275.1 4.0 copy-start.1
  309.5 17.5 %collective-permute-start = (bf16[64,512]{1,0:T(8,128)(2,1)S(1)}, bf16[64,512]{1,0:T(8,128)(2,1)S(1)}, u32[]{:S(2)}, u32[]{:S(2)}) collective-permute-start(bf16[64,512]{1,0:T(8,128)(2,1)S(1)} %maximum_select_fusion.2), channel_id=1, source_target_pairs={{0,8},{8,16},{16,24},{1,9},{9,17},{17,25},{2,10},{10,18},{18,26},{... | collective-permute-start | bytes 196616 | tf_op jit(solution)/shard_map/while/body/eval_jaxpr/ppermute | solution.py:14
  327.0 29.7 %copy-start = (bf16[4096,512]{1,0:T(8,128)(2,1)S(1)}, bf16[4096,512]{1,0:T(8,128)(2,1)}, u32[]{:S(2)}) copy-start(bf16[4096,512]{1,0:T(8,128)(2,1)} %get-tuple-element.579) | copy-start | bytes 12582916 | tf_op jit(solution)/shard_map/while
  353.5 4.0 copy-start.1
  388.1 17.8 %collective-permute-start = (bf16[64,512]{1,0:T(8,128)(2,1)S(1)}, bf16[64,512]{1,0:T(8,128)(2,1)S(1)}, u32[]{:S(2)}, u32[]{:S(2)}) collective-permute-start(bf16[64,512]{1,0:T(8,128)(2,1)S(1)} %maximum_select_fusion.2), channel_id=1, source_target_pairs={{0,8},{8,16},{16,24},{1,9},{9,17},{17,25},{2,10},{10,18},{18,26},{... | collective-permute-start | bytes 196616 | tf_op jit(solution)/shard_map/while/body/eval_jaxpr/ppermute | solution.py:14
  405.9 0.6 copy-start.2
